TPU v7x, 32 devices: a whole 2x2x4 slice. The times are simulated.
32 devices in a mesh: grp: 2 (over y), src: 4 (over z), chan: 2 (over x), row: 2 (over core).
Axes of the slice: x: 2, y: 2, z: 4, core: 2. Of those that a mesh axis runs over, the one named last changes fastest.
Arguments:
- features: bfloat16 [64, 128, 512], P('chan', ('grp', 'row'), 'src'), parts along dimension 1, may hold values from -6 to 6
- layout: int32 [128, 512], P(('grp', 'row'), 'chan'), parts along dimension 0, may hold values 0 or 1
- conv_weight: bfloat16 [4, 4, 9, 64, 64], P('src'), may hold values from -0.25 to 0.25
- conv_bias: float32 [4, 4, 64], P('src'), may hold values from -2 to 2
- head_weight: bfloat16 [4, 64, 16], P('src'), may hold values from -0.75 to 0.75
- transmission: float32 [4, 16], P('src'), may hold values from -3 to 3
- point_weight: float32 [128], replicated, may hold values from 0.1 to 1
- assignment: int32 [128, 1], replicated, may hold values from 0 to 3
Outputs:
- intensity: float32 [8, 4, 32, 512], P(None, ('grp', 'row'), 'src', 'chan'), parts along dimension 1
There are 2 independent parts, one for each index of `grp`. A program takes and returns all parts, laid end to end along the dimension named above; an argument that names none is the same for every part. Nothing has to cross between parts.
Inputs may be any that keep to these rules, and one draw needn't show every extreme that they name: `assignment`: every cluster is named by at least one point.
All inputs are finite; a program needn't handle non-finite values. No bound on the sum of `layout` on one device may be relied on, other than what follows from the above.
Results may differ from a plain program's by a relative error of at most 0.009.
Values may be sent and summed in bfloat16 or wider, within the bound.
A program may use at most 64 MiB of HBM per device.

v0:
```python
import functools
import math

import jax
import jax.numpy as jnp
from jax import lax
from jax.experimental import pallas as pl
from jax.experimental.pallas import tpu as pltpu
from jax.sharding import PartitionSpec as P


def with_halo(block, sides, width):
    for axis, dim in sides:
        count = lax.axis_size(axis)
        forward = [(i, i + 1) for i in range(count - 1)]
        backward = [(target, source) for source, target in forward]
        low = lax.ppermute(
            lax.slice_in_dim(block, block.shape[dim] - width, None, axis=dim), axis, forward
        )
        high = lax.ppermute(lax.slice_in_dim(block, 0, width, axis=dim), axis, backward)
        block = jnp.concatenate([low, block, high], axis=dim)
    return block


def advance(core_cells, padded, weights, biases, dilation):
    tile_rows, tile_cols = (core_cells.shape[1], core_cells.shape[2])
    kernel = weights.reshape(3, 3, weights.shape[1], weights.shape[2])
    window = padded[:, : tile_rows + 2 * dilation, : tile_cols + 2 * dilation]
    summed = lax.conv_general_dilated(
        window[None],
        kernel,
        (1, 1),
        "VALID",
        rhs_dilation=(dilation, dilation),
        dimension_numbers=("NCHW", "HWIO", "NCHW"),
        preferred_element_type=jnp.float32,
    )[0]
    summed = summed + biases[:, None, None]
    return (core_cells.astype(jnp.float32) + jax.nn.gelu(summed, approximate=True)).astype(
        jnp.bfloat16
    )


def by_cluster(
    features, layout, conv_weight, conv_bias, head_weight, transmission, point_weight, assignment
):
    channels = lax.all_gather(features, "chan", axis=0, tiled=True)
    full_cache = lax.all_gather(channels, "src", axis=2, tiled=True)
    column_width = full_cache.shape[2] // lax.axis_size("chan")
    tile_cache = lax.dynamic_slice_in_dim(
        full_cache, lax.axis_index("chan") * column_width, column_width, 2
    )
    weights = conv_weight[0]
    biases = conv_bias[0]
    hidden = tile_cache
    for layer_index in range(weights.shape[0]):
        dilation = 2**layer_index
        padded = with_halo(hidden, (("chan", 2), ("row", 1)), dilation)
        hidden = advance(hidden, padded, weights[layer_index], biases[layer_index], dilation)
    field_map = jnp.einsum(
        "ihw,ik->khw", hidden, head_weight[0], preferred_element_type=jnp.float32
    )
    field_map = field_map + layout.astype(jnp.float32)[None] * transmission[0][:, None, None]
    planes = field_map.shape[0] // 2
    power_map = field_map[:planes] ** 2 + field_map[planes:] ** 2
    chosen = assignment[:, 0] == lax.axis_index("src")
    cluster_share = jnp.sum(jnp.where(chosen, point_weight, jnp.zeros((), jnp.float32))) / jnp.sum(
        point_weight
    )
    summed = lax.psum_scatter(
        (power_map * cluster_share).astype(jnp.bfloat16), "src", scatter_dimension=1, tiled=True
    ).astype(jnp.float32)
    return summed[:, None]


def gelu_of_half(v):
    c = 2.0 * math.sqrt(2.0 / math.pi)
    return v + v * jnp.tanh(v * (c + (c * 4.0 * 0.044715) * (v * v)))


def beside(h, d):
    n, rows, lanes = h.shape
    zero = jnp.zeros((n, 8, lanes), h.dtype)
    tiles = [h[:, 8 * g : 8 * g + 8] for g in range(rows // 8)]
    low = lax.broadcasted_iota(jnp.int32, zero.shape, 2) < lanes // 2
    if d % 8 == 0:
        up = tiles[d // 8 :] + [zero] * (d // 8)
        down = [zero] * (d // 8) + tiles[: -(d // 8)]
        return jnp.concatenate([jnp.where(low, a, b) for a, b in zip(up, down)], axis=1)
    sub = lax.broadcasted_iota(jnp.int32, zero.shape, 1)
    inner = jnp.where(low, sub, 7 - sub) < 8 - d
    up = [pltpu.roll(v, 8 - d, 1) for v in tiles] + [zero]
    down = [zero] + [pltpu.roll(v, d, 1) for v in tiles]
    out = []
    for g in range(len(tiles)):
        near = jnp.where(low, up[g], down[g + 1])
        far = jnp.where(low, up[g + 1], down[g])
        out.append(jnp.where(inner, near, far))
    return jnp.concatenate(out, axis=1)


def repair(h, d):
    shape = h.shape
    h = h.reshape(-1, 8, shape[2])
    sub = lax.broadcasted_iota(jnp.int32, h.shape, 1)
    half = lax.broadcasted_iota(jnp.int32, h.shape, 2) // (shape[2] // 2)
    bit = (sub // d) % 2
    other = pltpu.roll(h, shape[2] // 2, 2)
    swapped = jnp.where(bit == 1, pltpu.roll(other, d, 1), pltpu.roll(other, 8 - d, 1))
    return jnp.where(bit == half, h, swapped).reshape(shape)


def chunks_of(groups, d, rows):
    best = 1
    for g in range(1, groups + 1):
        if groups % g == 0 and g * d * rows <= 512:
            best = g
    return best


MESH = pl.DeviceIdType.MESH


def xor(s, k):
    total = s
    bit = 1
    while bit <= k:
        if k & bit:
            total = total + bit - 2 * bit * ((s // bit) % 2)
        bit *= 2
    return total


def pixel_kernel(
    layers, n_src, t_ref, w_ref, h_ref, tr_ref, b_ref, m_ref, pw_ref, as_ref, o_ref, *scratch
):
    bufs = scratch[: layers + 1]
    got, wraw, pbuf, mbuf, wide, acc, obuf = scratch[layers + 1 : layers + 8]
    fs, fr, es, er, ws, wr, vs, vr, ps, pr, ms, mr, os, orr, lw = scratch[layers + 8 :]
    s, c, r = (lax.axis_index(a) for a in ("src", "chan", "row"))
    halo = 2**layers - 1
    lanes = t_ref.shape[2]
    half_rows = t_ref.shape[1]
    rows = 2 * half_rows
    piece = t_ref.shape[0] // 8
    here = 2 * c + r
    side = c

    ch = lanes // 2
    planes2 = h_ref.shape[0]
    ia = lax.broadcasted_iota(jnp.int32, (planes2, planes2), 0)
    ib = lax.broadcasted_iota(jnp.int32, (planes2, planes2), 1)
    column = jnp.sum(jnp.where(ia == ib, tr_ref[...], 0.0), axis=1, keepdims=True)
    pbuf[0, :planes2, :] = jnp.concatenate(
        [h_ref[...].astype(jnp.float32), jnp.broadcast_to(column, (planes2, ch))], axis=1)
    bias_half = 0.5 * b_ref[...]
    pbuf[0, planes2 : planes2 + layers, :] = jnp.concatenate([bias_half, bias_half], axis=1)

    barrier = pltpu.get_barrier_semaphore()
    for s1 in range(n_src):
        for c1 in range(2):
            for r1 in range(2):
                @pl.when(jnp.logical_not((s == s1) & (c == c1) & (r == r1)))
                def _():
                    pl.semaphore_signal(
                        barrier, inc=1, device_id={"src": s1, "chan": c1, "row": r1},
                        device_id_type=MESH,
                    )
    pl.semaphore_wait(barrier, 4 * n_src - 1)

    def remote(src, dst, a, b, s1, c1, r1):
        return pltpu.make_async_remote_copy(
            src_ref=src, dst_ref=dst, send_sem=a, recv_sem=b,
            device_id={"src": s1, "chan": c1, "row": r1}, device_id_type=MESH,
        )

    def main_copy(c1, r1):
        return (
            t_ref.at[pl.ds(piece * (3 * c1 + 2 * r1), 3 * piece)],
            got.at[here, pl.ds(piece * (1 - c1), 3 * piece)],
        )

    def edge_copy(c1, r1):
        at = 7 * (1 - c1) if c1 == r1 else 1 + 5 * c1
        return t_ref.at[pl.ds(piece * at, piece)], got.at[here, pl.ds(piece * 3 * c1, piece)]

    def each(act):
        for c1 in (0, 1):
            for r1 in (0, 1):
                k = 2 * c1 + r1
                me = (c == c1) & (r == r1)
                act(c1, r1, k, me)

    def send_main(c1, r1, k, me):
        src, dst = main_copy(c1, r1)
        pl.when(jnp.logical_not(me))(
            lambda: remote(src, dst, fs.at[k], fr.at[here], s, c1, r1).start())
        pl.when(me)(lambda: pltpu.make_async_copy(src, dst, fr.at[here]).start())

    def edge_step(c1):
        return 1 - 2 * c1

    def send_edge(c1, r1, k, me):
        src, dst = edge_copy(c1, r1)
        if c1 == r1:
            s1 = s + edge_step(c1)
            pl.when((s1 >= 0) & (s1 < n_src))(
                lambda: remote(src, dst, es.at[k], er.at[here], s1, c1, r1).start())
        else:
            pl.when(jnp.logical_not(me))(
                lambda: remote(src, dst, es.at[k], er.at[here], s, c1, r1).start())
            pl.when(me)(lambda: pltpu.make_async_copy(src, dst, er.at[here]).start())

    def send_mask(c1, r1, k, me):
        src, dst = m_ref.at[k], mbuf.at[r]
        owner = c == (2 * s) // n_src
        pl.when(owner & jnp.logical_not(me))(
            lambda: remote(src, dst, ms.at[k], mr.at[r], s, c1, r1).start())
        pl.when(owner & me)(lambda: pltpu.make_async_copy(src, dst, mr.at[r]).start())

    each(send_main)
    each(send_edge)

    def wz(k):
        return remote(w_ref.at[r], wraw.at[k, r], ws.at[k], wr.at[k], xor(s, k), c, r)

    def pz(k):
        return remote(pbuf.at[0], pbuf.at[k], ps.at[k], pr.at[k], xor(s, k), c, r)

    for k in range(1, n_src):
        pz(k).start()
        wz(k).start()
    each(send_mask)
    own_w = pltpu.make_async_copy(w_ref, wraw.at[0], lw)
    own_w.start()

    wide[...] = jnp.zeros_like(wide)
    outside = ((here == 0) & (s == 0)) | ((here == 3) & (s == n_src - 1))

    @pl.when(outside)
    def _():
        for k in range(4):
            got[k, pl.ds(piece * 3 * side, piece)] = jnp.zeros((piece,) + got.shape[2:], got.dtype)

    def build(k):
        low = lax.broadcasted_iota(jnp.int32, (ch, lanes), 1) < ch
        per = layers // 2
        for l in range(layers):
            raw = lambda i: wraw[k, l // per, (l % per) * 5 + i].astype(jnp.float32) * 0.5
            firsts = [raw(b) for b in range(3)]
            q0, q1 = raw(3), raw(4)
            seconds = [q0, pltpu.roll(q0, ch, 1), q1]
            for b in range(3):
                w10, w2 = firsts[b], seconds[b]
                swap = pltpu.roll(w10, ch, 1)
                blocks = [
                    w10,
                    jnp.where(low, w2, swap),
                    jnp.where(low, 0.0, pltpu.roll(w2, ch, 1)),
                    jnp.where(low, swap, 0.0),
                ]
                for j in range(4):
                    v = blocks[j].astype(wide.dtype)
                    for ic in range(2):
                        at = (b + ic) * 4 * ch + j * ch
                        wide[l, at : at + ch, ic * lanes : (ic + 1) * lanes] = v

    own_w.wait()
    build(0)

    def wait_main(c1, r1, k, me):
        src, _ = main_copy(0, 0)
        dst = got.at[k, pl.ds(piece * (1 - side), 3 * piece)]
        pl.when(jnp.logical_not(me))(
            lambda: remote(src, dst, fs.at[k], fr.at[k], s, c1, r1).wait_recv())
        pl.when(me)(lambda: pltpu.make_async_copy(src, dst, fr.at[k]).wait())

    def wait_edge(c1, r1, k, me):
        src, _ = edge_copy(0, 0)
        dst = got.at[k, pl.ds(piece * 3 * side, piece)]
        far = c == r
        inside = jnp.logical_not(outside)
        pl.when(jnp.where(far, inside, jnp.logical_not(me)))(
            lambda: remote(src, dst, es.at[k], er.at[k], s, c1, r1).wait_recv())
        pl.when(jnp.logical_not(far) & me)(
            lambda: pltpu.make_async_copy(src, dst, er.at[k]).wait())

    each(wait_main)
    each(wait_edge)
    n_in = 2 * t_ref.shape[0] // 4 + 2 * halo
    q = ch // 2
    rin = lax.broadcasted_iota(jnp.int32, (2 * lanes, 2 * lanes), 0)
    rout = lax.broadcasted_iota(jnp.int32, (2 * lanes, 2 * lanes), 1)
    want = (rout // q % 2) * lanes + (rout // lanes) * ch + (rout // ch % 2) * q + rout % q
    place = jnp.where(rin == want, 1.0, 0.0).astype(t_ref.dtype)
    strips = []
    for r1 in range(2):
        pairs = got.shape[1]
        lhs = jnp.concatenate(
            [got[2 * c1 + r1].reshape(pairs * half_rows, lanes) for c1 in range(2)], axis=1)
        v = jnp.dot(lhs, place, preferred_element_type=jnp.float32)
        v = v.reshape(pairs, half_rows, 2 * lanes)
        parts = []
        for t in range(pairs):
            parts += [v[t : t + 1, :, :lanes], v[t : t + 1, :, lanes:]]
        skip = (2 * pairs - n_in) // 2
        strips.append(jnp.concatenate(parts[skip : skip + n_in], axis=0))
    x = jnp.concatenate(strips, axis=1)
    bufs[0][:, :, :lanes] = x.astype(jnp.bfloat16)
    bufs[0][:, :, lanes:] = beside(x, 1).astype(jnp.bfloat16)

    own_cols = n_in - 2 * halo
    at_left = (here == 0) & (s == 0)
    at_right = (here == 3) & (s == n_src - 1)
    for r1 in range(2):
        for_self = (c == (2 * s) // n_src) & (r == r1)
        pl.when(jnp.logical_not(for_self))(
            lambda: remote(m_ref.at[0], mbuf.at[r1], ms.at[0], mr.at[r1], s, c, r).wait_recv())
        pl.when(for_self)(
            lambda: pltpu.make_async_copy(m_ref.at[0], mbuf.at[r1], mr.at[r1]).wait())

    def share_copy(k):
        return remote(wraw.at[k, r], wraw.at[k, r], vs.at[k], vr.at[k], s, c, 1 - r)

    total = jnp.sum(pw_ref[...], axis=1, keepdims=True)

    def compute(k, cid):
        share = jnp.sum(jnp.where(as_ref[...] == cid, pw_ref[...], 0.0), axis=1, keepdims=True) / total
        margin = 0
        for l in range(layers):
            d = 2**l
            src = bufs[l]
            n_out = src.shape[0] - 2 * d
            margin += d
            groups = n_out // (2 * d)
            per = chunks_of(groups, d, rows)
            if l == layers - 2 and k + 1 < n_src:
                wz(k + 1).wait_recv()
                share_copy(k + 1).start()
            bias = pbuf[k, 2 * q2 + l : 2 * q2 + l + 1, :]
            for chunk in range(groups // per):
                base = chunk * per * 2 * d
                lhs = jnp.concatenate(
                    [
                        jnp.concatenate(
                            [src[base + 2 * d * g + j * d : base + 2 * d * g + (j + 1) * d] for g in range(per)],
                            axis=0,
                        ).reshape(per * d * rows, 2 * lanes)
                        for j in range(4)
                    ],
                    axis=1,
                )
                out = jnp.dot(lhs, wide[l], preferred_element_type=jnp.float32)
                out = out.reshape(per * d, rows, 2 * lanes)
                parts = []
                for g in range(per):
                    parts += [out[g * d : (g + 1) * d, :, :lanes], out[g * d : (g + 1) * d, :, lanes:]]
                z = jnp.concatenate(parts, axis=0) + bias[None]
                n = per * 2 * d
                centre = src[base + d : base + d + n, :, :lanes].astype(jnp.float32)
                h = centre + gelu_of_half(z)
                edge = halo - margin
                left = min(max(edge - base, 0), n)
                right = min(max(base + n - (n_out - edge), 0), n - left)
                if left or right:
                    cut = [h[left : n - right]]
                    if left:
                        cut.insert(0, jnp.where(at_left, 0.0, h[:left]))
                    if right:
                        cut.append(jnp.where(at_right, 0.0, h[n - right :]))
                    h = jnp.concatenate(cut, axis=0)
                if l + 1 < layers:
                    h = repair(h, d)
                    bufs[l + 1][base : base + n, :, :lanes] = h.astype(jnp.bfloat16)
                    bufs[l + 1][base : base + n, :, lanes:] = beside(h, 2 * d).astype(jnp.bfloat16)
                else:
                    bufs[l + 1][base * rows : (base + n) * rows] = h.reshape(n * rows, lanes)
        final = bufs[layers]
        head = pbuf[k, : 2 * q2, :]
        low = lax.broadcasted_iota(jnp.int32, head.shape, 1) < ch
        h_lo = jnp.where(low, head, 0.0)
        h_hi = jnp.where(low, 0.0, pltpu.roll(head, ch, 1))
        tcol = head[:, ch : ch + 1]
        hw = jnp.concatenate([h_lo[:q2], h_hi[:q2], h_lo[q2:], h_hi[q2:]], axis=0).astype(jnp.bfloat16)
        tr = jnp.concatenate([tcol[:q2], tcol[:q2], tcol[q2:], tcol[q2:]], axis=0)
        for g in range(rows // 8):
            block = jnp.concatenate(
                [final[pl.ds(g * 8 + b, own_cols, stride=rows), :] for b in range(8)], axis=0
            ).astype(jnp.bfloat16)
            field = lax.dot_general(
                hw, block, (((1,), (1,)), ((), ())), preferred_element_type=jnp.float32)
            m = mbuf[g // 2, 2 * (g % 2) : 2 * (g % 2) + 2]
            mm = jnp.concatenate(
                [jnp.broadcast_to(m[i : i + 1], (q2, m.shape[1])) for i in (0, 1, 0, 1)], axis=0)
            field = field + mm * tr
            power = (field[: 2 * q2] ** 2 + field[2 * q2 :] ** 2) * share
            if k == 0:
                acc[g] = power
            else:
                acc[g] = acc[g] + power

    q2 = acc.shape[1] // 2
    for k in range(n_src):
        if k > 0:
            remote(
                wraw.at[k, 1 - r], wraw.at[k, 1 - r], vs.at[k], vr.at[k], s, c, 1 - r
            ).wait_recv()
            pz(k).wait_recv()
            build(k)
        compute(k, xor(s, k))

    c2 = (2 * s) // n_src
    slot = 4 * (s % 2) + here

    def outgoing(act):
        for s1 in range(n_src):
            for r1 in range(2):
                k = 2 * s1 + r1
                src = acc.at[2 * r1 + s1 // 2, pl.ds((s1 % 2) * q2, q2)]
                me = (s == s1) & (c == c2) & (r == r1)
                act(s1, r1, k, src, me)

    def send_out(s1, r1, k, src, me):
        dst = obuf.at[slot]
        pl.when(jnp.logical_not(me))(
            lambda: remote(src, dst, os.at[k], orr.at[slot], s1, c2, r1).start())
        pl.when(me)(lambda: pltpu.make_async_copy(src, dst, orr.at[slot]).start())

    outgoing(send_out)
    mine = c == c2
    for k in range(2 * n_src):
        me = mine & (slot == k)
        src = acc.at[0, pl.ds(0, q2)]
        pl.when(jnp.logical_not(me))(
            lambda: remote(src, obuf.at[k], os.at[k], orr.at[k], s, c, r).wait_recv())
        pl.when(me)(lambda: pltpu.make_async_copy(src, obuf.at[k], orr.at[k]).wait())
    for b in range(8):
        o_ref[:, b, :] = jnp.concatenate(
            [obuf[k, :, b * own_cols : (b + 1) * own_cols] for k in range(2 * n_src)], axis=1)

    def sent_main(c1, r1, k, me):
        src, dst = main_copy(c1, r1)
        pl.when(jnp.logical_not(me))(
            lambda: remote(src, dst, fs.at[k], fr.at[here], s, c1, r1).wait_send())

    def sent_edge(c1, r1, k, me):
        src, dst = edge_copy(c1, r1)
        s1 = s + edge_step(c1)
        gone = (s1 >= 0) & (s1 < n_src) if c1 == r1 else jnp.logical_not(me)
        pl.when(gone)(lambda: remote(src, dst, es.at[k], er.at[here], s, c1, r1).wait_send())

    def sent_mask(c1, r1, k, me):
        owner = c == (2 * s) // n_src
        pl.when(owner & jnp.logical_not(me))(
            lambda: remote(m_ref.at[k], mbuf.at[r], ms.at[k], mr.at[r], s, c1, r1).wait_send())

    def sent_out(s1, r1, k, src, me):
        pl.when(jnp.logical_not(me))(
            lambda: remote(src, obuf.at[slot], os.at[k], orr.at[slot], s1, c2, r1).wait_send())

    each(sent_main)
    each(sent_edge)
    each(sent_mask)
    outgoing(sent_out)
    for k in range(1, n_src):
        pz(k).wait_send()
        wz(k).wait_send()
        share_copy(k).wait_send()


def by_pixel(
    features, layout, conv_weight, conv_bias, head_weight, transmission, point_weight, assignment
):
    n_src, n_chan, n_row = (lax.axis_size(a) for a in ("src", "chan", "row"))
    s = lax.axis_index("src")
    layers = conv_weight.shape[1]
    halo = 2**layers - 1
    part, strip, block = features.shape
    ch = part * n_chan
    width = block * n_src
    rows = strip * n_row // 2
    own = block // (n_chan * n_row)
    lanes = 2 * ch
    d_last = 2 ** (layers - 1)
    pairs = features.reshape(part, strip // 2, 2, block // 2, 2).transpose(3, 1, 4, 2, 0)
    pairs = pairs.reshape(block // 2, strip // 2, lanes)
    w = conv_weight[0].reshape(layers, 3, 3, ch, ch)
    zero = jnp.zeros((layers, ch, ch), w.dtype)
    packed = [jnp.concatenate([w[:, 1, b], w[:, 0, b]], -1) for b in range(3)]
    packed.append(jnp.concatenate([w[:, 2, 0], w[:, 2, 1]], -1))
    packed.append(jnp.concatenate([w[:, 2, 2], zero], -1))
    packed = jnp.stack(packed, 1).reshape(2, layers // 2 * 5, ch, lanes)
    planes2 = head_weight.shape[2]
    half_tile = layout.shape[1] // block
    mask = lax.dynamic_slice_in_dim(layout, (s % half_tile) * block, block, 1).astype(jnp.float32)
    mask = mask.reshape(strip // (2 * d_last), 2, d_last, 4, own).transpose(3, 0, 1, 2, 4)
    mask = mask.reshape(4, strip // d_last, d_last * own)
    spec = lambda shape, kind=jnp.bfloat16: pltpu.VMEM(shape, kind)
    scratch = []
    n = own + 2 * halo
    for l in range(layers):
        scratch.append(spec((n, rows, 2 * lanes)))
        n -= 2 * 2**l
    scratch.append(spec((n * rows, lanes), jnp.float32))
    groups = rows // d_last
    scratch += [
        spec((4, block // 4, rows // 2, lanes)),
        spec((n_src,) + packed.shape),
        spec((n_src, planes2 + (layers + 7) // 8 * 8, lanes), jnp.float32),
        spec((2,) + mask.shape[1:], jnp.float32),
        spec((layers, 16 * ch, 2 * lanes)),
        spec((groups, planes2, own * d_last), jnp.float32),
        spec((2 * n_src, planes2 // 2, own * d_last), jnp.float32),
    ]
    dma = pltpu.SemaphoreType.DMA
    for count in (4, 4, 4, 4, n_src, n_src, n_src, n_src, n_src, n_src, 4, 2, 2 * n_src, 2 * n_src):
        scratch.append(dma((count,)))
    scratch += [dma(())]
    vmem = pl.BlockSpec(memory_space=pltpu.VMEM)
    out = pl.pallas_call(
        functools.partial(pixel_kernel, layers, n_src),
        out_shape=jax.ShapeDtypeStruct((planes2 // 2, d_last, width // n_chan), jnp.float32),
        in_specs=[vmem] * 8,
        out_specs=vmem,
        scratch_shapes=scratch,
        compiler_params=pltpu.CompilerParams(
            vmem_limit_bytes=56 * 2**20, collective_id=0, has_side_effects=True),
    )(pairs, packed, head_weight[0].T, transmission, conv_bias[0], mask, point_weight[None], assignment.reshape(1, -1))
    return out[:, None]


def solution(mesh):
    in_specs = (
        P("chan", ("grp", "row"), "src"),
        P(("grp", "row"), "chan"),
        P("src", None, None, None, None),
        P("src", None, None),
        P("src", None, None),
        P("src", None),
        P(),
        P(),
    )
    out_specs = P(None, ("grp", "row"), "src", "chan")

    def shards(*args):
        features, weights = args[0], args[2]
        halo = 2 ** weights.shape[1] - 1
        own = features.shape[2] // (mesh.shape["chan"] * mesh.shape["row"])
        fits = own >= 2 * halo and mesh.shape["chan"] == mesh.shape["row"] == 2
        body = by_pixel if fits and mesh.shape["src"] == 4 else by_cluster
        return body(*args)

    return jax.shard_map(shards, mesh=mesh, in_specs=in_specs, out_specs=out_specs, check_vma=False)
```

profile of v0, /device:TPU:0, one launch (start us, length us, event | category | flops | bytes accessed | tf_op | source)
XLA Modules:
  0.0 42.5 jit_solution(15367461729884013127)
XLA Ops:
  0.0 1.5 %copy.21 = bf16[32,32,128]{0,2,1:T(8,128)(2,1)S(1)} copy(bf16[32,32,128]{2,1,0:T(8,128)(2,1)} %param.8) | data formatting | bytes 524288 | tf_op args[0]
  1.5 0.7 %copy.22 = bf16[64,16,2,2,32]{0,4,3,2,1:T(8,128)(2,1)S(1)} copy(bf16[64,16,2,2,32]{4,2,0,3,1:T(2,128)(2,1)S(1)} %bitcast.74) | data formatting | bytes 524288 | tf_op jit(solution)/shard_map/transpose | solution.py:485
  2.2 0.0 copy-start
  2.2 1.0 %copy.33.t_ref = bf16[64,16,128]{2,1,0:T(8,128)(2,1)} copy(bf16[64,16,128]{0,2,1:T(8,128)(2,1)S(1)} %bitcast.75) | data formatting | bytes 524288 | tf_op jit(solution)/shard_map/reshape | solution.py:486
  3.2 0.1 copy-done
  3.3 0.1 fusion
  3.4 0.1 fusion.1
  3.5 0.1 fusion.2
  3.6 0.1 fusion.3
  3.8 0.0 copy-start.1
  3.8 0.0 copy-start.2
  3.8 0.8 %copy-done.2 = s32[32,256]{1,0:T(8,128)S(1)} copy-done((s32[32,256]{1,0:T(8,128)S(1)}, s32[32,256]{1,0:T(8,128)}, u32[]{:S(2)}) %copy-start.2) | copy-done | bytes 32792
  4.6 0.1 reshape.21
  4.7 0.7 %reshape.22.m_ref = f32[4,4,256]{2,1,0:T(4,128)} reshape(f32[4,2,2,8,32]{4,3,2,1,0:T(8,128)S(1)} %bitcast.79) | data formatting | bytes 32768 | tf_op jit(solution)/shard_map/reshape | solution.py:497
  5.4 0.0 copy-done.1
  5.4 35.7 %shard_map.82 = f32[8,8,256]{2,1,0:T(8,128)} custom-call(bf16[64,16,128]{2,1,0:T(8,128)(2,1)} %copy.33.t_ref, bf16[2,10,64,128]{3,2,1,0:T(8,128)(2,1)} %bitcast.77, bf16[16,64]{1,0:T(8,128)(2,1)} %bitcast.80, f32[1,16]{1,0:T(1,128)} %tr_ref.1, f32[4,64]{1,0:T(4,128)} %bitcast.81, f32[4,4,256]{2,1,0:T(4,128)} %reshape.22.m_ref, f32[1,128]{1,0:T(1,128)} %bitcast.82, ...), custom_call_target="tpu_custom_call" | custom-call | tf_op jit(solution)/shard_map/pallas_call | solution.py:520
  41.1 1.5 %copy.51 = f32[8,1,8,256]{3,2,1,0:T(8,128)} copy(f32[8,1,8,256]{3,2,1,0:T(8,128)} %bitcast.78) | data formatting | bytes 131072
  (4 shorter events, 0.1 us)
Async XLA Ops:
  2.2 1.1 %copy-start = (bf16[1,4,9,64,64]{4,3,2,1,0:T(8,128)(2,1)S(1)}, bf16[1,4,9,64,64]{4,3,2,1,0:T(8,128)(2,1)}, u32[]{:S(2)}) copy-start(bf16[1,4,9,64,64]{4,3,2,1,0:T(8,128)(2,1)} %param.10) | copy-start | bytes 884740
  3.8 1.6 %copy-start.1 = (bf16[4,5,64,128]{3,2,1,0:T(8,128)(2,1)}, bf16[4,5,64,128]{3,2,1,0:T(8,128)(2,1)S(1)}, u32[]{:S(2)}) copy-start(bf16[4,5,64,128]{3,2,1,0:T(8,128)(2,1)S(1)} %bitcast_dynamic-update-slice_fusion) | copy-start | bytes 983044
  3.8 0.8 %copy-start.2 = (s32[32,256]{1,0:T(8,128)S(1)}, s32[32,256]{1,0:T(8,128)}, u32[]{:S(2)}) copy-start(s32[32,256]{1,0:T(8,128)} %param.9) | copy-start | bytes 98308
where the time goes:
time: 42.9 us; the launch traced here: 42.5 us
  Pallas kernels  35.7 us (83%)
  local copies, waits for them, and re-layouts  6.34 us (15%)
    pallas_call x1, Pallas kernels, by_pixel(): pl.pallas_call(functools.partial(pixel_kernel, layers, n_src), out_shape=...  35.7 us
    unnamed x8, local copies, waits for them, and re-layouts  3.81 us
    reshape x1, local copies, waits for them, and re-layouts, by_pixel(): pairs = pairs.reshape(block // 2, strip // 2, lanes)  0.96 us

commit v1 on v0

--- a/solution.py
+++ b/solution.py
@@ -78,47 +78,42 @@
     return v + v * jnp.tanh(v * (c + (c * 4.0 * 0.044715) * (v * v)))
 
 
-def beside(h, d):
-    n, rows, lanes = h.shape
-    zero = jnp.zeros((n, 8, lanes), h.dtype)
-    tiles = [h[:, 8 * g : 8 * g + 8] for g in range(rows // 8)]
-    low = lax.broadcasted_iota(jnp.int32, zero.shape, 2) < lanes // 2
-    if d % 8 == 0:
-        up = tiles[d // 8 :] + [zero] * (d // 8)
-        down = [zero] * (d // 8) + tiles[: -(d // 8)]
-        return jnp.concatenate([jnp.where(low, a, b) for a, b in zip(up, down)], axis=1)
-    sub = lax.broadcasted_iota(jnp.int32, zero.shape, 1)
-    inner = jnp.where(low, sub, 7 - sub) < 8 - d
-    up = [pltpu.roll(v, 8 - d, 1) for v in tiles] + [zero]
-    down = [zero] + [pltpu.roll(v, d, 1) for v in tiles]
+def half_lanes(shape):
+    return lax.broadcasted_iota(jnp.int32, shape, len(shape) - 1) < shape[-1] // 2
+
+
+def pair_up(h, d, segs):
+    n, sub, lanes = h.shape
+    low = half_lanes((1, sub, lanes))
+    if d * segs < sub:
+        first = lax.broadcasted_iota(jnp.int32, (1, sub, lanes), 1) < sub // 2
+        other = pltpu.roll(pltpu.roll(h, sub // 2, 1), lanes // 2, 2)
+        return jnp.where(first == low, h, other)
+    g = d * segs // sub
+    turned = pltpu.roll(h, lanes // 2, 2)
+    groups = n // g
+    at = lambda x, m: x[m * g : (m + 1) * g]
     out = []
-    for g in range(len(tiles)):
-        near = jnp.where(low, up[g], down[g + 1])
-        far = jnp.where(low, up[g + 1], down[g])
-        out.append(jnp.where(inner, near, far))
-    return jnp.concatenate(out, axis=1)
-
-
-def repair(h, d):
-    shape = h.shape
-    h = h.reshape(-1, 8, shape[2])
-    sub = lax.broadcasted_iota(jnp.int32, h.shape, 1)
-    half = lax.broadcasted_iota(jnp.int32, h.shape, 2) // (shape[2] // 2)
-    bit = (sub // d) % 2
-    other = pltpu.roll(h, shape[2] // 2, 2)
-    swapped = jnp.where(bit == 1, pltpu.roll(other, d, 1), pltpu.roll(other, 8 - d, 1))
-    return jnp.where(bit == half, h, swapped).reshape(shape)
-
-
-def chunks_of(groups, d, rows):
-    best = 1
-    for g in range(1, groups + 1):
-        if groups % g == 0 and g * d * rows <= 512:
-            best = g
-    return best
+    for i in range((groups + 2) // 2):
+        u, v = 2 * i - 1, 2 * i
+        if i == 0:
+            out += [at(turned, v), at(h, v)]
+        elif v == groups:
+            out += [at(h, u), at(turned, u)]
+        else:
+            out += [jnp.where(low, at(h, u), at(turned, v)), jnp.where(low, at(turned, u), at(h, v))]
+    return jnp.concatenate(out, axis=0)
+
+
+def shift_segment(h, segs, down):
+    sub = lax.broadcasted_iota(jnp.int32, (1,) + h.shape[1:], 1) % segs
+    if down:
+        return jnp.where(sub == 0, 0.0, pltpu.roll(h, 1, 1))
+    return jnp.where(sub == segs - 1, 0.0, pltpu.roll(h, h.shape[1] - 1, 1))
 
 
 MESH = pl.DeviceIdType.MESH
+CHUNKS = 2
 
 
 def xor(s, k):
@@ -134,14 +129,13 @@
 def pixel_kernel(
     layers, n_src, t_ref, w_ref, h_ref, tr_ref, b_ref, m_ref, pw_ref, as_ref, o_ref, *scratch
 ):
-    bufs = scratch[: layers + 1]
-    got, wraw, pbuf, mbuf, wide, acc, obuf = scratch[layers + 1 : layers + 8]
-    fs, fr, es, er, ws, wr, vs, vr, ps, pr, ms, mr, os, orr, lw = scratch[layers + 8 :]
+    first, bufs = scratch[0], (scratch[1 : layers + 1], scratch[layers + 1 : 2 * layers + 1])
+    got, wraw, pbuf, mbuf, wide, acc, sbuf, obuf, stage, rowbuf = scratch[2 * layers + 1 : 2 * layers + 11]
+    fs, fr, es, er, ws, wr, vs, vr, ps, pr, ms, mr, os, orr, lw = scratch[2 * layers + 11 :]
     s, c, r = (lax.axis_index(a) for a in ("src", "chan", "row"))
-    halo = 2**layers - 1
     lanes = t_ref.shape[2]
     half_rows = t_ref.shape[1]
-    rows = 2 * half_rows
+    rows = 4 * half_rows
     piece = t_ref.shape[0] // 8
     here = 2 * c + r
     side = c
@@ -234,7 +228,10 @@
     own_w = pltpu.make_async_copy(w_ref, wraw.at[0], lw)
     own_w.start()
 
-    wide[...] = jnp.zeros_like(wide)
+    for k in range(n_src):
+        for l in range(layers):
+            for at, cut in ((0, lanes), (12 * ch, 0)):
+                wide[k, l, at : at + 4 * ch, cut : cut + lanes] = jnp.zeros((4 * ch, lanes), wide.dtype)
     outside = ((here == 0) & (s == 0)) | ((here == 3) & (s == n_src - 1))
 
     @pl.when(outside)
@@ -263,7 +260,7 @@
                     v = blocks[j].astype(wide.dtype)
                     for ic in range(2):
                         at = (b + ic) * 4 * ch + j * ch
-                        wide[l, at : at + ch, ic * lanes : (ic + 1) * lanes] = v
+                        wide[k, l, at : at + ch, ic * lanes : (ic + 1) * lanes] = v
 
     own_w.wait()
     build(0)
@@ -287,29 +284,48 @@
 
     each(wait_main)
     each(wait_edge)
-    n_in = 2 * t_ref.shape[0] // 4 + 2 * halo
     q = ch // 2
+    span = 2**layers
+    segs = rows // span
+    slots = got.shape[1]
+    own_cols = 2 * slots - 2 * span
     rin = lax.broadcasted_iota(jnp.int32, (2 * lanes, 2 * lanes), 0)
     rout = lax.broadcasted_iota(jnp.int32, (2 * lanes, 2 * lanes), 1)
-    want = (rout // q % 2) * lanes + (rout // lanes) * ch + (rout // ch % 2) * q + rout % q
+    want = (rout // q % 2) * lanes + (rout // ch % 2) * ch + (rout // lanes) * q + rout % q
     place = jnp.where(rin == want, 1.0, 0.0).astype(t_ref.dtype)
-    strips = []
     for r1 in range(2):
-        pairs = got.shape[1]
         lhs = jnp.concatenate(
-            [got[2 * c1 + r1].reshape(pairs * half_rows, lanes) for c1 in range(2)], axis=1)
+            [got[2 * c1 + r1].reshape(slots * half_rows, lanes) for c1 in range(2)], axis=1)
         v = jnp.dot(lhs, place, preferred_element_type=jnp.float32)
-        v = v.reshape(pairs, half_rows, 2 * lanes)
-        parts = []
-        for t in range(pairs):
-            parts += [v[t : t + 1, :, :lanes], v[t : t + 1, :, lanes:]]
-        skip = (2 * pairs - n_in) // 2
-        strips.append(jnp.concatenate(parts[skip : skip + n_in], axis=0))
-    x = jnp.concatenate(strips, axis=1)
-    bufs[0][:, :, :lanes] = x.astype(jnp.bfloat16)
-    bufs[0][:, :, lanes:] = beside(x, 1).astype(jnp.bfloat16)
-
-    own_cols = n_in - 2 * halo
+        for yp in range(2):
+            stage[2 * r1 + yp] = v[:, yp * lanes : (yp + 1) * lanes]
+    mrows = slots * segs
+    rowbuf[0:8, :] = jnp.zeros((8, lanes), jnp.float32)
+    rowbuf[8 + span * mrows : 16 + span * mrows, :] = jnp.zeros((8, lanes), jnp.float32)
+    for r1 in range(2):
+        for y2 in range(half_rows):
+            for yp in range(2):
+                y = 2 * y2 + yp
+                at = 8 + (y % span) * mrows + r1 * (segs // 2) + y // span
+                rowbuf[pl.ds(at, slots, stride=segs), :] = stage[
+                    2 * r1 + yp, pl.ds(y2, slots, stride=half_rows), :]
+    low_lanes = half_lanes((1, 8, lanes))
+    as_tiles = lambda v: v.reshape(-1, 8, lanes)
+    for y in range(span):
+        at = 8 + y * mrows
+        own = as_tiles(rowbuf[at : at + mrows, :])
+        near = jnp.where(
+            low_lanes, as_tiles(rowbuf[at + segs : at + segs + mrows, :]),
+            as_tiles(rowbuf[at - segs : at - segs + mrows, :]))
+        places = [(y, own, near)]
+        if y == span - 1:
+            places.append((-1, shift_segment(own, segs, True), shift_segment(near, segs, True)))
+        if y == 0:
+            places.append((span, shift_segment(own, segs, False), shift_segment(near, segs, False)))
+        for yy, a, b in places:
+            first[yy + 1, :, :lanes] = a.reshape(mrows, lanes).astype(first.dtype)
+            first[yy + 1, :, lanes:] = b.reshape(mrows, lanes).astype(first.dtype)
+
     at_left = (here == 0) & (s == 0)
     at_right = (here == 3) & (s == n_src - 1)
     for r1 in range(2):
@@ -324,58 +340,53 @@
 
     total = jnp.sum(pw_ref[...], axis=1, keepdims=True)
 
-    def compute(k, cid):
+    def store_next(dst, h, y, d):
+        wider = 2 * d
+        places = [(y, h)]
+        if y >= span - wider:
+            places.append((y - span, shift_segment(h, segs, True)))
+        if y < wider:
+            places.append((y + span, shift_segment(h, segs, False)))
+        for yy, v in places:
+            v = pair_up(v, d, segs)
+            n = v.shape[0]
+            out = (slots // 2 - own_cols // 4) * segs // 8
+            v = jnp.concatenate(
+                [jnp.where(at_left, 0.0, v[:out]), v[out : n - out], jnp.where(at_right, 0.0, v[n - out :])],
+                axis=0)
+            g = wider * segs // 8
+            near = jnp.where(low_lanes, v[2 * g :], v[: n - 2 * g])
+            own = v[g : n - g]
+            dst[yy + wider, :, :lanes] = own.reshape(-1, lanes).astype(dst.dtype)
+            dst[yy + wider, :, lanes:] = near.reshape(-1, lanes).astype(dst.dtype)
+
+    def multiply(k, l, ys):
+        d = 2**l
+        src = first if l == 0 else bufs[k % 2][l - 1]
+        lhs = jnp.concatenate(
+            [jnp.concatenate([src[y + j * d] for y in ys], axis=0) for j in range(4)], axis=1)
+        return jnp.dot(lhs, wide[k, l], preferred_element_type=jnp.float32)
+
+    def activate(k, l, ys, out):
+        d = 2**l
+        src = first if l == 0 else bufs[k % 2][l - 1]
+        dst = bufs[k % 2][l]
+        n = src.shape[1]
+        bias = pbuf[k, 2 * q2 + l : 2 * q2 + l + 1, :]
+        for i, y in enumerate(ys):
+            for e in range(2):
+                z = out[i * n : (i + 1) * n, e * lanes : (e + 1) * lanes] + bias
+                yy = y + e * d
+                h = src[yy + d, :, :lanes].astype(jnp.float32) + gelu_of_half(z)
+                if l + 1 < layers:
+                    store_next(dst, h.reshape(-1, 8, lanes), yy, d)
+                else:
+                    dst[yy * n : (yy + 1) * n, :] = h
+
+    def finish(k, cid):
         share = jnp.sum(jnp.where(as_ref[...] == cid, pw_ref[...], 0.0), axis=1, keepdims=True) / total
-        margin = 0
-        for l in range(layers):
-            d = 2**l
-            src = bufs[l]
-            n_out = src.shape[0] - 2 * d
-            margin += d
-            groups = n_out // (2 * d)
-            per = chunks_of(groups, d, rows)
-            if l == layers - 2 and k + 1 < n_src:
-                wz(k + 1).wait_recv()
-                share_copy(k + 1).start()
-            bias = pbuf[k, 2 * q2 + l : 2 * q2 + l + 1, :]
-            for chunk in range(groups // per):
-                base = chunk * per * 2 * d
-                lhs = jnp.concatenate(
-                    [
-                        jnp.concatenate(
-                            [src[base + 2 * d * g + j * d : base + 2 * d * g + (j + 1) * d] for g in range(per)],
-                            axis=0,
-                        ).reshape(per * d * rows, 2 * lanes)
-                        for j in range(4)
-                    ],
-                    axis=1,
-                )
-                out = jnp.dot(lhs, wide[l], preferred_element_type=jnp.float32)
-                out = out.reshape(per * d, rows, 2 * lanes)
-                parts = []
-                for g in range(per):
-                    parts += [out[g * d : (g + 1) * d, :, :lanes], out[g * d : (g + 1) * d, :, lanes:]]
-                z = jnp.concatenate(parts, axis=0) + bias[None]
-                n = per * 2 * d
-                centre = src[base + d : base + d + n, :, :lanes].astype(jnp.float32)
-                h = centre + gelu_of_half(z)
-                edge = halo - margin
-                left = min(max(edge - base, 0), n)
-                right = min(max(base + n - (n_out - edge), 0), n - left)
-                if left or right:
-                    cut = [h[left : n - right]]
-                    if left:
-                        cut.insert(0, jnp.where(at_left, 0.0, h[:left]))
-                    if right:
-                        cut.append(jnp.where(at_right, 0.0, h[n - right :]))
-                    h = jnp.concatenate(cut, axis=0)
-                if l + 1 < layers:
-                    h = repair(h, d)
-                    bufs[l + 1][base : base + n, :, :lanes] = h.astype(jnp.bfloat16)
-                    bufs[l + 1][base : base + n, :, lanes:] = beside(h, 2 * d).astype(jnp.bfloat16)
-                else:
-                    bufs[l + 1][base * rows : (base + n) * rows] = h.reshape(n * rows, lanes)
-        final = bufs[layers]
+        final = bufs[k % 2][layers - 1]
+        n = final.shape[0] // span
         head = pbuf[k, : 2 * q2, :]
         low = lax.broadcasted_iota(jnp.int32, head.shape, 1) < ch
         h_lo = jnp.where(low, head, 0.0)
@@ -383,13 +394,15 @@
         tcol = head[:, ch : ch + 1]
         hw = jnp.concatenate([h_lo[:q2], h_hi[:q2], h_lo[q2:], h_hi[q2:]], axis=0).astype(jnp.bfloat16)
         tr = jnp.concatenate([tcol[:q2], tcol[:q2], tcol[q2:], tcol[q2:]], axis=0)
+        per = rows // 16
         for g in range(rows // 8):
+            at = 8 * (g % 2) * n + g // 2
             block = jnp.concatenate(
-                [final[pl.ds(g * 8 + b, own_cols, stride=rows), :] for b in range(8)], axis=0
+                [final[pl.ds(at + b * n, n // segs, stride=segs), :] for b in range(8)], axis=0
             ).astype(jnp.bfloat16)
             field = lax.dot_general(
                 hw, block, (((1,), (1,)), ((), ())), preferred_element_type=jnp.float32)
-            m = mbuf[g // 2, 2 * (g % 2) : 2 * (g % 2) + 2]
+            m = mbuf[g // per, 2 * (g % per) : 2 * (g % per) + 2]
             mm = jnp.concatenate(
                 [jnp.broadcast_to(m[i : i + 1], (q2, m.shape[1])) for i in (0, 1, 0, 1)], axis=0)
             field = field + mm * tr
@@ -399,15 +412,57 @@
             else:
                 acc[g] = acc[g] + power
 
-    q2 = acc.shape[1] // 2
-    for k in range(n_src):
-        if k > 0:
-            remote(
-                wraw.at[k, 1 - r], wraw.at[k, 1 - r], vs.at[k], vr.at[k], s, c, 1 - r
-            ).wait_recv()
-            pz(k).wait_recv()
-            build(k)
-        compute(k, xor(s, k))
+    q2 = h_ref.shape[0] // 2
+
+    def take(k):
+        wz(k).wait_recv()
+        share_copy(k).start()
+
+    def receive(k):
+        remote(
+            wraw.at[k, 1 - r], wraw.at[k, 1 - r], vs.at[k], vr.at[k], s, c, 1 - r
+        ).wait_recv()
+        pz(k).wait_recv()
+        build(k)
+
+    take(1)
+    receive(1)
+    for k0 in range(0, n_src, 2):
+        pending = None
+        for l in range(layers):
+            d = 2**l
+            tops = [y for y in range(span) if y % (2 * d) < d]
+            step = len(tops) // CHUNKS
+            for k in (k0, k0 + 1):
+                for i in range(CHUNKS):
+                    ys = tops[i * step : (i + 1) * step]
+                    out = multiply(k, l, ys)
+                    if pending:
+                        activate(*pending)
+                    pending = (k, l, ys, out)
+            if k0 + 2 < n_src and l == layers - 2:
+                for k in (k0 + 2, k0 + 3):
+                    take(k)
+        activate(*pending)
+        for k in (k0, k0 + 1):
+            finish(k, xor(s, k))
+        if k0 + 2 < n_src:
+            for k in (k0 + 2, k0 + 3):
+                receive(k)
+
+    pin = lax.broadcasted_iota(jnp.int32, (2 * lanes, 2 * lanes), 0)
+    pout = lax.broadcasted_iota(jnp.int32, (2 * lanes, 2 * lanes), 1)
+    column = pout % own_cols
+    half = span // 2
+    source = (
+        (column // half % 2) * lanes + pout // own_cols * (own_cols // 2)
+        + column // span * half + column % half)
+    order = jnp.where(pin == source, 1.0, 0.0).astype(jnp.bfloat16)
+    both = jnp.concatenate(
+        [jnp.concatenate([acc[g, :q2], acc[g, q2:]], axis=1) for g in range(rows // 8)], axis=0)
+    sbuf[...] = jnp.dot(
+        both.astype(jnp.bfloat16), order, preferred_element_type=jnp.float32
+    ).reshape(sbuf.shape)
 
     c2 = (2 * s) // n_src
     slot = 4 * (s % 2) + here
@@ -416,7 +471,7 @@
         for s1 in range(n_src):
             for r1 in range(2):
                 k = 2 * s1 + r1
-                src = acc.at[2 * r1 + s1 // 2, pl.ds((s1 % 2) * q2, q2)]
+                src = sbuf.at[n_src * r1 + s1]
                 me = (s == s1) & (c == c2) & (r == r1)
                 act(s1, r1, k, src, me)
 
@@ -430,7 +485,7 @@
     mine = c == c2
     for k in range(2 * n_src):
         me = mine & (slot == k)
-        src = acc.at[0, pl.ds(0, q2)]
+        src = sbuf.at[0]
         pl.when(jnp.logical_not(me))(
             lambda: remote(src, obuf.at[k], os.at[k], orr.at[k], s, c, r).wait_recv())
         pl.when(me)(lambda: pltpu.make_async_copy(src, obuf.at[k], orr.at[k]).wait())
@@ -474,17 +529,16 @@
     n_src, n_chan, n_row = (lax.axis_size(a) for a in ("src", "chan", "row"))
     s = lax.axis_index("src")
     layers = conv_weight.shape[1]
-    halo = 2**layers - 1
     part, strip, block = features.shape
     ch = part * n_chan
     width = block * n_src
-    rows = strip * n_row // 2
+    rows = strip * n_row
     own = block // (n_chan * n_row)
     lanes = 2 * ch
-    d_last = 2 ** (layers - 1)
+    span = 2**layers
     pairs = features.reshape(part, strip // 2, 2, block // 2, 2).transpose(3, 1, 4, 2, 0)
     pairs = pairs.reshape(block // 2, strip // 2, lanes)
-    w = conv_weight[0].reshape(layers, 3, 3, ch, ch)
+    w = conv_weight[0].reshape(layers, 3, 3, ch, ch).transpose(0, 2, 1, 3, 4)
     zero = jnp.zeros((layers, ch, ch), w.dtype)
     packed = [jnp.concatenate([w[:, 1, b], w[:, 0, b]], -1) for b in range(3)]
     packed.append(jnp.concatenate([w[:, 2, 0], w[:, 2, 1]], -1))
@@ -493,24 +547,29 @@
     planes2 = head_weight.shape[2]
     half_tile = layout.shape[1] // block
     mask = lax.dynamic_slice_in_dim(layout, (s % half_tile) * block, block, 1).astype(jnp.float32)
-    mask = mask.reshape(strip // (2 * d_last), 2, d_last, 4, own).transpose(3, 0, 1, 2, 4)
-    mask = mask.reshape(4, strip // d_last, d_last * own)
+    mask = mask.reshape(strip // 8, 8, 4, own // span, 2, span // 2).transpose(2, 0, 4, 1, 3, 5)
+    mask = mask.reshape(4, strip // 4, 4 * own)
     spec = lambda shape, kind=jnp.bfloat16: pltpu.VMEM(shape, kind)
     scratch = []
-    n = own + 2 * halo
-    for l in range(layers):
-        scratch.append(spec((n, rows, 2 * lanes)))
-        n -= 2 * 2**l
-    scratch.append(spec((n * rows, lanes), jnp.float32))
-    groups = rows // d_last
+    slots = block // 4
+    segs = rows // span
+    scratch.append(spec((span + 2, slots * segs, 2 * lanes)))
+    for _ in range(2):
+        for l in range(1, layers):
+            scratch.append(spec((span + 2 * 2**l, (slots - 2 * 2**l) * segs, 2 * lanes)))
+        scratch.append(spec((span * (slots - span) * segs, lanes), jnp.float32))
+    groups = rows // 8
     scratch += [
-        spec((4, block // 4, rows // 2, lanes)),
+        spec((4, slots, strip // 2, lanes)),
         spec((n_src,) + packed.shape),
         spec((n_src, planes2 + (layers + 7) // 8 * 8, lanes), jnp.float32),
         spec((2,) + mask.shape[1:], jnp.float32),
-        spec((layers, 16 * ch, 2 * lanes)),
-        spec((groups, planes2, own * d_last), jnp.float32),
-        spec((2 * n_src, planes2 // 2, own * d_last), jnp.float32),
+        spec((n_src, layers, 16 * ch, 2 * lanes)),
+        spec((groups, planes2, lanes), jnp.float32),
+        spec((groups, planes2 // 2, 8 * own), jnp.float32),
+        spec((2 * n_src, planes2 // 2, 8 * own), jnp.float32),
+        spec((4, slots * strip // 2, lanes), jnp.float32),
+        spec((span * slots * segs + 16, lanes), jnp.float32),
     ]
     dma = pltpu.SemaphoreType.DMA
     for count in (4, 4, 4, 4, n_src, n_src, n_src, n_src, n_src, n_src, 4, 2, 2 * n_src, 2 * n_src):
@@ -519,7 +578,7 @@
     vmem = pl.BlockSpec(memory_space=pltpu.VMEM)
     out = pl.pallas_call(
         functools.partial(pixel_kernel, layers, n_src),
-        out_shape=jax.ShapeDtypeStruct((planes2 // 2, d_last, width // n_chan), jnp.float32),
+        out_shape=jax.ShapeDtypeStruct((planes2 // 2, 8, width // n_chan), jnp.float32),
         in_specs=[vmem] * 8,
         out_specs=vmem,
         scratch_shapes=scratch,

time: 42.9 us -> 43.5 us (1.014)
  local copies, waits for them, and re-layouts: 6.34 us -> 7.12 us
    reshape x3, local copies, waits for them, and re-layouts: 0.79 us -> 1.52 us  [the longest x1 0.97 us: by_pixel(): mask = mask.reshape(4, strip // 4, 4 * own)]
where the time goes in v1:
time: 43.5 us; the launch traced here: 43.2 us
  Pallas kernels  35.5 us (82%)
  local copies, waits for them, and re-layouts  7.12 us (16%)
    pallas_call x1, Pallas kernels, by_pixel(): pl.pallas_call(functools.partial(pixel_kernel, layers, n_src), out_shape=...  35.5 us
    unnamed x8, local copies, waits for them, and re-layouts  3.81 us
    reshape x1, local copies, waits for them, and re-layouts, by_pixel(): mask = mask.reshape(4, strip // 4, 4 * own)  0.97 us
    reshape x1, local copies, waits for them, and re-layouts, by_pixel(): pairs = pairs.reshape(block // 2, strip // 2, lanes)  0.96 us

profile of v1, /device:TPU:0, one launch (start us, length us, event | category | flops | bytes accessed | tf_op | source)
XLA Modules:
  0.0 43.2 jit_solution(14465424061170679088)
XLA Ops:
  0.0 1.5 %copy.17 = bf16[32,32,128]{0,2,1:T(8,128)(2,1)S(1)} copy(bf16[32,32,128]{2,1,0:T(8,128)(2,1)} %param.8) | data formatting | bytes 524288 | tf_op args[0]
  1.5 0.7 %copy.18 = bf16[64,16,2,2,32]{0,4,3,2,1:T(8,128)(2,1)S(1)} copy(bf16[64,16,2,2,32]{4,2,0,3,1:T(2,128)(2,1)S(1)} %bitcast.65) | data formatting | bytes 524288 | tf_op jit(solution)/shard_map/transpose | solution.py:539
  2.2 0.0 copy-start
  2.2 1.0 %copy.25.t_ref = bf16[64,16,128]{2,1,0:T(8,128)(2,1)} copy(bf16[64,16,128]{0,2,1:T(8,128)(2,1)S(1)} %bitcast.67) | data formatting | bytes 524288 | tf_op jit(solution)/shard_map/reshape | solution.py:540
  3.2 0.1 copy-done
  3.3 0.1 slice_bitcast_fusion
  3.4 0.1 fusion
  3.5 0.1 fusion.1
  3.6 0.1 fusion.2
  3.7 0.1 fusion.3
  3.8 0.0 copy-start.1
  3.8 0.0 copy-start.2
  3.9 0.8 %copy-done.2 = s32[32,256]{1,0:T(8,128)S(1)} copy-done((s32[32,256]{1,0:T(8,128)S(1)}, s32[32,256]{1,0:T(8,128)}, u32[]{:S(2)}) %copy-start.2) | copy-done | bytes 32792
  4.6 0.4 reshape.21
  5.1 0.1 copy.30
  5.2 0.0 copy-done.1
  5.2 1.0 %reshape.22.m_ref = f32[4,8,128]{2,1,0:T(8,128)} reshape(f32[4,4,2,8,2,8]{5,4,3,2,1,0:T(2,128)S(1)} %bitcast.68) | data formatting | bytes 32768 | tf_op jit(solution)/shard_map/reshape | solution.py:551
  6.2 35.5 %shard_map.82 = f32[8,8,256]{2,1,0:T(8,128)} custom-call(bf16[64,16,128]{2,1,0:T(8,128)(2,1)} %copy.25.t_ref, bf16[2,10,64,128]{3,2,1,0:T(8,128)(2,1)} %bitcast.70, bf16[16,64]{1,0:T(8,128)(2,1)} %bitcast.72, f32[1,16]{1,0:T(1,128)} %tr_ref.1, f32[4,64]{1,0:T(4,128)} %bitcast.73, f32[4,8,128]{2,1,0:T(8,128)} %reshape.22.m_ref, f32[1,128]{1,0:T(1,128)} %bitcast.74, ...), custom_call_target="tpu_custom_call" | custom-call | tf_op jit(solution)/shard_map/pallas_call | solution.py:579
  41.7 1.5 %copy.36 = f32[8,1,8,256]{3,2,1,0:T(8,128)} copy(f32[8,1,8,256]{3,2,1,0:T(8,128)} %bitcast.71) | data formatting | bytes 131072
  (3 shorter events, 0.1 us)
Async XLA Ops:
  2.2 1.1 %copy-start = (bf16[1,4,9,64,64]{4,3,2,1,0:T(8,128)(2,1)S(1)}, bf16[1,4,9,64,64]{4,3,2,1,0:T(8,128)(2,1)}, u32[]{:S(2)}) copy-start(bf16[1,4,9,64,64]{4,3,2,1,0:T(8,128)(2,1)} %param.10) | copy-start | bytes 884740
  3.8 1.4 %copy-start.1 = (bf16[4,5,64,128]{3,2,1,0:T(8,128)(2,1)}, bf16[4,5,64,128]{3,2,1,0:T(8,128)(2,1)S(1)}, u32[]{:S(2)}) copy-start(bf16[4,5,64,128]{3,2,1,0:T(8,128)(2,1)S(1)} %bitcast_dynamic-update-slice_fusion) | copy-start | bytes 983044
  3.8 0.8 %copy-start.2 = (s32[32,256]{1,0:T(8,128)S(1)}, s32[32,256]{1,0:T(8,128)}, u32[]{:S(2)}) copy-start(s32[32,256]{1,0:T(8,128)} %param.9) | copy-start | bytes 98308

commit v2 on v1

--- a/solution.py
+++ b/solution.py
@@ -127,28 +127,18 @@
 
 
 def pixel_kernel(
-    layers, n_src, t_ref, w_ref, h_ref, tr_ref, b_ref, m_ref, pw_ref, as_ref, o_ref, *scratch
+    layers, n_src, f_ref, w_ref, h_ref, tr_ref, b_ref, y_ref, pw_ref, as_ref, o_ref, *scratch
 ):
     first, bufs = scratch[0], (scratch[1 : layers + 1], scratch[layers + 1 : 2 * layers + 1])
-    got, wraw, pbuf, mbuf, wide, acc, sbuf, obuf, stage, rowbuf = scratch[2 * layers + 1 : 2 * layers + 11]
-    fs, fr, es, er, ws, wr, vs, vr, ps, pr, ms, mr, os, orr, lw = scratch[2 * layers + 11 :]
-    s, c, r = (lax.axis_index(a) for a in ("src", "chan", "row"))
+    got, wraw, pbuf, mbuf, wide, acc, sbuf, obuf, stage, rowbuf, t_ref, m_ref = scratch[2 * layers + 1 : 2 * layers + 13]
+    fs, fr, es, er, ws, wr, ys, yr, vs, vr, ps, pr, ms, mr, os, orr = scratch[2 * layers + 13 :]
+    gp, s, c, r = (lax.axis_index(a) for a in ("grp", "src", "chan", "row"))
     lanes = t_ref.shape[2]
     half_rows = t_ref.shape[1]
     rows = 4 * half_rows
     piece = t_ref.shape[0] // 8
     here = 2 * c + r
     side = c
-
-    ch = lanes // 2
-    planes2 = h_ref.shape[0]
-    ia = lax.broadcasted_iota(jnp.int32, (planes2, planes2), 0)
-    ib = lax.broadcasted_iota(jnp.int32, (planes2, planes2), 1)
-    column = jnp.sum(jnp.where(ia == ib, tr_ref[...], 0.0), axis=1, keepdims=True)
-    pbuf[0, :planes2, :] = jnp.concatenate(
-        [h_ref[...].astype(jnp.float32), jnp.broadcast_to(column, (planes2, ch))], axis=1)
-    bias_half = 0.5 * b_ref[...]
-    pbuf[0, planes2 : planes2 + layers, :] = jnp.concatenate([bias_half, bias_half], axis=1)
 
     barrier = pltpu.get_barrier_semaphore()
     for s1 in range(n_src):
@@ -160,7 +150,51 @@
                         barrier, inc=1, device_id={"src": s1, "chan": c1, "row": r1},
                         device_id_type=MESH,
                     )
-    pl.semaphore_wait(barrier, 4 * n_src - 1)
+    pl.semaphore_signal(barrier, inc=1, device_id={"grp": 1 - gp}, device_id_type=MESH)
+    ch = lanes // 2
+    planes2 = h_ref.shape[0]
+    ia = lax.broadcasted_iota(jnp.int32, (planes2, planes2), 0)
+    ib = lax.broadcasted_iota(jnp.int32, (planes2, planes2), 1)
+    column = jnp.sum(jnp.where(ia == ib, tr_ref[...], 0.0), axis=1, keepdims=True)
+    pbuf[0, :planes2, :] = jnp.concatenate(
+        [h_ref[...].astype(jnp.float32), jnp.broadcast_to(column, (planes2, ch))], axis=1)
+    bias_half = 0.5 * b_ref[...]
+    pbuf[0, planes2 : planes2 + layers, :] = jnp.concatenate([bias_half, bias_half], axis=1)
+
+    part, strip, block = f_ref.shape
+    for ci in range(part):
+        rowbuf[ci * strip : (ci + 1) * strip, :] = f_ref[ci].astype(jnp.float32)
+    kin = lax.broadcasted_iota(jnp.int32, (block // 2, 2 * block), 1)
+    kout = lax.broadcasted_iota(jnp.int32, (block // 2, 2 * block), 0)
+    pick = jnp.where(kin % block == 2 * kout + kin // block, 1.0, 0.0).astype(jnp.bfloat16)
+    blank = jnp.zeros((2 * part, block), jnp.bfloat16)
+    base = part * strip
+    for y4 in range(strip // 4):
+        cells = []
+        for y2 in (2 * y4, 2 * y4 + 1):
+            both_rows = jnp.concatenate(
+                [rowbuf[pl.ds(2 * y2 + yp, part, stride=strip), :] for yp in range(2)], axis=0
+            ).astype(jnp.bfloat16)
+            cells.append(jnp.concatenate([both_rows, blank], axis=1))
+            cells.append(jnp.concatenate([blank, both_rows], axis=1))
+        moved = lax.dot_general(
+            pick, jnp.concatenate(cells, axis=0), (((1,), (1,)), ((), ())),
+            preferred_element_type=jnp.float32)
+        for e in range(2):
+            rowbuf[pl.ds(base + 2 * y4 + e, block // 2, stride=half_rows), :] = moved[
+                :, e * lanes : (e + 1) * lanes]
+    for x8 in range(block // 16):
+        t_ref[8 * x8 : 8 * x8 + 8] = rowbuf[
+            base + 8 * x8 * half_rows : base + 8 * (x8 + 1) * half_rows, :
+        ].reshape(8, half_rows, lanes).astype(t_ref.dtype)
+
+    per = layers // 2
+    for l in range(layers):
+        for i, (one, two) in enumerate(((1, 0), (4, 3), (7, 6), (2, 5), (8, None))):
+            other = jnp.zeros((ch, ch), w_ref.dtype) if two is None else w_ref[l, two]
+            wraw[0, l // per, (l % per) * 5 + i] = jnp.concatenate([w_ref[l, one], other], axis=1)
+
+    pl.semaphore_wait(barrier, 4 * n_src)
 
     def remote(src, dst, a, b, s1, c1, r1):
         return pltpu.make_async_remote_copy(
@@ -215,8 +249,18 @@
     each(send_main)
     each(send_edge)
 
+    blocks = wraw.shape[2] // 2
+
     def wz(k):
-        return remote(w_ref.at[r], wraw.at[k, r], ws.at[k], wr.at[k], xor(s, k), c, r)
+        at = pl.ds(gp * blocks, blocks)
+        return remote(wraw.at[0, r, at], wraw.at[k, r, at], ws.at[k], wr.at[k], xor(s, k), c, r)
+
+    def wy(k, g1):
+        piece_of = wraw.at[k, r, pl.ds(g1 * blocks, blocks)]
+        return pltpu.make_async_remote_copy(
+            src_ref=piece_of, dst_ref=piece_of, send_sem=ys.at[k], recv_sem=yr.at[k],
+            device_id={"grp": 1 - gp}, device_id_type=MESH,
+        )
 
     def pz(k):
         return remote(pbuf.at[0], pbuf.at[k], ps.at[k], pr.at[k], xor(s, k), c, r)
@@ -224,9 +268,25 @@
     for k in range(1, n_src):
         pz(k).start()
         wz(k).start()
+    column = pl.multiple_of((s % (y_ref.shape[1] // block)) * block, block)
+    wanted = y_ref[:, pl.ds(column, block)].astype(jnp.bfloat16)
+    unit = half_rows // 2
+    xin = lax.broadcasted_iota(jnp.int32, (block, block), 0)
+    xout = lax.broadcasted_iota(jnp.int32, (block, block), 1)
+    from_x = xout // (4 * unit) * (4 * unit) + (xout // unit % 2) * 2 * unit + (xout // (2 * unit) % 2) * unit + xout % unit
+    sorted_x = jnp.dot(
+        wanted, jnp.where(xin == from_x, 1.0, 0.0).astype(jnp.bfloat16), preferred_element_type=jnp.float32)
+    seg_of = lax.broadcasted_iota(jnp.int32, (8, block), 1) // (block // 8)
+    sub_of = lax.broadcasted_iota(jnp.int32, (8, block), 0)
+    for g in range(strip // 8):
+        tile = sorted_x[8 * g : 8 * g + 8]
+        turned = tile
+        for e in range(1, 8):
+            moved = pltpu.roll(pltpu.roll(tile, 8 - e, 0), e * block // 8, 1)
+            turned = jnp.where((seg_of - sub_of + 8) % 8 == e, moved, turned)
+        for kt in range(4):
+            m_ref[kt, 2 * g : 2 * g + 2, :] = turned[2 * kt : 2 * kt + 2]
     each(send_mask)
-    own_w = pltpu.make_async_copy(w_ref, wraw.at[0], lw)
-    own_w.start()
 
     for k in range(n_src):
         for l in range(layers):
@@ -262,7 +322,6 @@
                         at = (b + ic) * 4 * ch + j * ch
                         wide[k, l, at : at + ch, ic * lanes : (ic + 1) * lanes] = v
 
-    own_w.wait()
     build(0)
 
     def wait_main(c1, r1, k, me):
@@ -282,6 +341,11 @@
         pl.when(jnp.logical_not(far) & me)(
             lambda: pltpu.make_async_copy(src, dst, er.at[k]).wait())
 
+    def take(k):
+        wz(k).wait_recv()
+        wy(k, gp).start()
+
+    take(1)
     each(wait_main)
     each(wait_edge)
     q = ch // 2
@@ -414,8 +478,8 @@
 
     q2 = h_ref.shape[0] // 2
 
-    def take(k):
-        wz(k).wait_recv()
+    def cross(k):
+        wy(k, 1 - gp).wait_recv()
         share_copy(k).start()
 
     def receive(k):
@@ -425,30 +489,38 @@
         pz(k).wait_recv()
         build(k)
 
-    take(1)
-    receive(1)
-    for k0 in range(0, n_src, 2):
-        pending = None
-        for l in range(layers):
-            d = 2**l
-            tops = [y for y in range(span) if y % (2 * d) < d]
-            step = len(tops) // CHUNKS
-            for k in (k0, k0 + 1):
-                for i in range(CHUNKS):
-                    ys = tops[i * step : (i + 1) * step]
-                    out = multiply(k, l, ys)
-                    if pending:
-                        activate(*pending)
-                    pending = (k, l, ys, out)
-            if k0 + 2 < n_src and l == layers - 2:
-                for k in (k0 + 2, k0 + 3):
-                    take(k)
-        activate(*pending)
-        for k in (k0, k0 + 1):
-            finish(k, xor(s, k))
-        if k0 + 2 < n_src:
-            for k in (k0 + 2, k0 + 3):
-                receive(k)
+    tops = lambda d: [y for y in range(span) if y % (2 * d) < d]
+    ahead = layers // 2
+    cross(1)
+    take(2)
+    pending = None
+    for step in range(ahead * (n_src + 1)):
+        k0, l0 = step // ahead, step % ahead
+        if l0 == 0 and 0 < k0 < n_src:
+            receive(k0)
+        if l0 == 0 and k0 + 1 < n_src and k0:
+            cross(k0 + 1)
+            if k0 + 2 < n_src:
+                take(k0 + 2)
+        for k, l in ((k0, l0), (k0 - 1, l0 + ahead)):
+            if not 0 <= k < n_src:
+                continue
+            ys_all = tops(2**l)
+            count = len(ys_all) // CHUNKS
+            for i in range(CHUNKS):
+                some = ys_all[i * count : (i + 1) * count]
+                if pending and pending[0] == k and pending[1] != l:
+                    activate(*pending)
+                    pending = None
+                out = multiply(k, l, some)
+                if pending:
+                    activate(*pending)
+                pending = (k, l, some, out)
+        if l0 == ahead - 1 and k0:
+            if pending[0] == k0 - 1:
+                activate(*pending)
+                pending = None
+            finish(k0 - 1, xor(s, k0 - 1))
 
     pin = lax.broadcasted_iota(jnp.int32, (2 * lanes, 2 * lanes), 0)
     pout = lax.broadcasted_iota(jnp.int32, (2 * lanes, 2 * lanes), 1)
@@ -520,6 +592,7 @@
     for k in range(1, n_src):
         pz(k).wait_send()
         wz(k).wait_send()
+        wy(k, gp).wait_send()
         share_copy(k).wait_send()
 
 
@@ -527,7 +600,6 @@
     features, layout, conv_weight, conv_bias, head_weight, transmission, point_weight, assignment
 ):
     n_src, n_chan, n_row = (lax.axis_size(a) for a in ("src", "chan", "row"))
-    s = lax.axis_index("src")
     layers = conv_weight.shape[1]
     part, strip, block = features.shape
     ch = part * n_chan
@@ -536,19 +608,7 @@
     own = block // (n_chan * n_row)
     lanes = 2 * ch
     span = 2**layers
-    pairs = features.reshape(part, strip // 2, 2, block // 2, 2).transpose(3, 1, 4, 2, 0)
-    pairs = pairs.reshape(block // 2, strip // 2, lanes)
-    w = conv_weight[0].reshape(layers, 3, 3, ch, ch).transpose(0, 2, 1, 3, 4)
-    zero = jnp.zeros((layers, ch, ch), w.dtype)
-    packed = [jnp.concatenate([w[:, 1, b], w[:, 0, b]], -1) for b in range(3)]
-    packed.append(jnp.concatenate([w[:, 2, 0], w[:, 2, 1]], -1))
-    packed.append(jnp.concatenate([w[:, 2, 2], zero], -1))
-    packed = jnp.stack(packed, 1).reshape(2, layers // 2 * 5, ch, lanes)
     planes2 = head_weight.shape[2]
-    half_tile = layout.shape[1] // block
-    mask = lax.dynamic_slice_in_dim(layout, (s % half_tile) * block, block, 1).astype(jnp.float32)
-    mask = mask.reshape(strip // 8, 8, 4, own // span, 2, span // 2).transpose(2, 0, 4, 1, 3, 5)
-    mask = mask.reshape(4, strip // 4, 4 * own)
     spec = lambda shape, kind=jnp.bfloat16: pltpu.VMEM(shape, kind)
     scratch = []
     slots = block // 4
@@ -561,20 +621,21 @@
     groups = rows // 8
     scratch += [
         spec((4, slots, strip // 2, lanes)),
-        spec((n_src,) + packed.shape),
+        spec((n_src, 2, layers // 2 * 5, ch, lanes)),
         spec((n_src, planes2 + (layers + 7) // 8 * 8, lanes), jnp.float32),
-        spec((2,) + mask.shape[1:], jnp.float32),
+        spec((2, strip // 4, block), jnp.float32),
         spec((n_src, layers, 16 * ch, 2 * lanes)),
         spec((groups, planes2, lanes), jnp.float32),
         spec((groups, planes2 // 2, 8 * own), jnp.float32),
         spec((2 * n_src, planes2 // 2, 8 * own), jnp.float32),
         spec((4, slots * strip // 2, lanes), jnp.float32),
         spec((span * slots * segs + 16, lanes), jnp.float32),
+        spec((block // 2, strip // 2, lanes)),
+        spec((4, strip // 4, block), jnp.float32),
     ]
     dma = pltpu.SemaphoreType.DMA
-    for count in (4, 4, 4, 4, n_src, n_src, n_src, n_src, n_src, n_src, 4, 2, 2 * n_src, 2 * n_src):
+    for count in (4, 4, 4, 4, n_src, n_src, n_src, n_src, n_src, n_src, n_src, n_src, 4, 2, 2 * n_src, 2 * n_src):
         scratch.append(dma((count,)))
-    scratch += [dma(())]
     vmem = pl.BlockSpec(memory_space=pltpu.VMEM)
     out = pl.pallas_call(
         functools.partial(pixel_kernel, layers, n_src),
@@ -583,8 +644,8 @@
         out_specs=vmem,
         scratch_shapes=scratch,
         compiler_params=pltpu.CompilerParams(
-            vmem_limit_bytes=56 * 2**20, collective_id=0, has_side_effects=True),
-    )(pairs, packed, head_weight[0].T, transmission, conv_bias[0], mask, point_weight[None], assignment.reshape(1, -1))
+            vmem_limit_bytes=26 * 2**20, collective_id=0, has_side_effects=True),
+    )(features, conv_weight[0], head_weight[0].T, transmission, conv_bias[0], layout, point_weight[None], assignment.reshape(1, -1))
     return out[:, None]
 
 
@@ -606,7 +667,7 @@
         halo = 2 ** weights.shape[1] - 1
         own = features.shape[2] // (mesh.shape["chan"] * mesh.shape["row"])
         fits = own >= 2 * halo and mesh.shape["chan"] == mesh.shape["row"] == 2
-        body = by_pixel if fits and mesh.shape["src"] == 4 else by_cluster
+        body = by_pixel if fits and mesh.shape["src"] == 4 and mesh.shape["grp"] == 2 else by_cluster
         return body(*args)
 
     return jax.shard_map(shards, mesh=mesh, in_specs=in_specs, out_specs=out_specs, check_vma=False)

time: 43.5 us -> 38.6 us (0.89)
  local copies, waits for them, and re-layouts: 7.12 us -> 4.11 us
  Pallas kernels: 35.5 us -> 34.2 us
    reshape x4 -> x0, local copies, waits for them, and re-layouts: 2.48 us -> none  [the longest x1 0.97 us: by_pixel(): mask = mask.reshape(4, strip // 4, 4 * own)]
    pallas_call x1, Pallas kernels: 35.5 us -> 34.2 us  [by_pixel(): pl.pallas_call(functools.partial(pixel_kernel, layers, n_src), out_shape=...]
    transpose x1 -> x0, local copies, waits for them, and re-layouts: 0.71 us -> none  [by_pixel(): features.reshape(part, strip // 2, 2, block // 2, 2)]
    unnamed x8 -> x17, local copies, waits for them, and re-layouts: 3.81 us -> 4.11 us
where the time goes in v2:
time: 38.6 us; the launch traced here: 38.3 us
  Pallas kernels  34.2 us (89%)
  local copies, waits for them, and re-layouts  4.11 us (11%)
    pallas_call x1, Pallas kernels, by_pixel(): pl.pallas_call(functools.partial(pixel_kernel, layers, n_src), out_shape=...  34.2 us
    unnamed x17, local copies, waits for them, and re-layouts  4.11 us

profile of v2, /device:TPU:0, one launch (start us, length us, event | category | flops | bytes accessed | tf_op | source)
XLA Modules:
  0.0 38.3 jit_solution(16771580365857160939)
XLA Ops:
  0.0 0.0 copy-start.3
  0.0 0.0 copy-start.4
  0.0 0.0 copy-start.5
  0.0 0.0 copy-start.6
  0.0 0.0 copy-start.7
  0.0 0.7 %copy-done.3 = bf16[1,64,16]{1,2,0:T(8,128)(2,1)S(1)} copy-done((bf16[1,64,16]{1,2,0:T(8,128)(2,1)S(1)}, bf16[1,64,16]{1,2,0:T(8,128)(2,1)}, u32[]{:S(2)}) %copy-start.3) | copy-done | bytes 2072
  0.7 0.0 copy-done.4
  0.7 0.0 copy-done.5
  0.7 0.0 copy-done.6
  0.7 0.0 copy-done.7
  0.7 0.0 copy-start
  0.7 1.1 %copy-done = bf16[1,4,9,64,64]{4,3,2,1,0:T(8,128)(2,1)S(1)} copy-done((bf16[1,4,9,64,64]{4,3,2,1,0:T(8,128)(2,1)S(1)}, bf16[1,4,9,64,64]{4,3,2,1,0:T(8,128)(2,1)}, u32[]{:S(2)}) %copy-start) | copy-done | bytes 294936
  1.8 0.0 copy-start.1
  1.8 0.9 %copy-done.1 = bf16[32,32,128]{2,1,0:T(8,128)(2,1)S(1)} copy-done((bf16[32,32,128]{2,1,0:T(8,128)(2,1)S(1)}, bf16[32,32,128]{2,1,0:T(8,128)(2,1)}, u32[]{:S(2)}) %copy-start.1) | copy-done | bytes 262168
  2.7 0.0 copy-start.2
  2.7 0.8 %copy-done.2 = s32[32,256]{1,0:T(8,128)S(1)} copy-done((s32[32,256]{1,0:T(8,128)S(1)}, s32[32,256]{1,0:T(8,128)}, u32[]{:S(2)}) %copy-start.2) | copy-done | bytes 32792
  3.5 34.2 %shard_map.82 = f32[8,8,256]{2,1,0:T(8,128)S(1)} custom-call(bf16[32,32,128]{2,1,0:T(8,128)(2,1)S(1)} %copy-done.1, bf16[4,9,64,64]{3,2,1,0:T(8,128)(2,1)S(1)} %bitcast.10, bf16[16,64]{1,0:T(8,128)(2,1)S(1)} %bitcast.12, f32[1,16]{1,0:T(1,128)S(1)} %copy-done.5, f32[4,64]{1,0:T(4,128)S(1)} %bitcast.13, s32[32,256]{1,0:T(8,128)S(1)} %copy-done.2, ...), custom_call_target="tpu_custom_call" | custom-call | tf_op jit(solution)/shard_map/pallas_call | solution.py:640
  37.7 0.6 %copy.11 = f32[8,1,8,256]{3,2,1,0:T(8,128)} copy(f32[8,1,8,256]{3,2,1,0:T(8,128)S(1)} %bitcast.11) | data formatting | bytes 131072
Async XLA Ops:
  0.0 0.7 %copy-start.3 = (bf16[1,64,16]{1,2,0:T(8,128)(2,1)S(1)}, bf16[1,64,16]{1,2,0:T(8,128)(2,1)}, u32[]{:S(2)}) copy-start(bf16[1,64,16]{1,2,0:T(8,128)(2,1)} %param.12) | copy-start | bytes 6148
  0.0 0.7 %copy-start.4 = (f32[1,4,64]{2,1,0:T(4,128)S(1)}, f32[1,4,64]{2,1,0:T(4,128)}, u32[]{:S(2)}) copy-start(f32[1,4,64]{2,1,0:T(4,128)} %param.11) | copy-start | bytes 3076
  0.0 0.7 %copy-start.5 = (f32[1,16]{1,0:T(1,128)S(1)}, f32[1,16]{1,0:T(1,128)}, u32[]{:S(2)}) copy-start(f32[1,16]{1,0:T(1,128)} %tr_ref.1) | copy-start | bytes 196
  0.0 0.7 %copy-start.6 = (f32[128]{0:T(128)S(1)}, f32[128]{0:T(128)}, u32[]{:S(2)}) copy-start(f32[128]{0:T(128)} %param.14) | copy-start | bytes 1540
  0.0 0.7 %copy-start.7 = (s32[128,1]{0,1:T(1,128)S(1)}, s32[128,1]{0,1:T(1,128)}, u32[]{:S(2)}) copy-start(s32[128,1]{0,1:T(1,128)} %param.15) | copy-start | bytes 1540
  0.7 1.1 %copy-start = (bf16[1,4,9,64,64]{4,3,2,1,0:T(8,128)(2,1)S(1)}, bf16[1,4,9,64,64]{4,3,2,1,0:T(8,128)(2,1)}, u32[]{:S(2)}) copy-start(bf16[1,4,9,64,64]{4,3,2,1,0:T(8,128)(2,1)} %param.10) | copy-start | bytes 884740
  1.8 0.9 %copy-start.1 = (bf16[32,32,128]{2,1,0:T(8,128)(2,1)S(1)}, bf16[32,32,128]{2,1,0:T(8,128)(2,1)}, u32[]{:S(2)}) copy-start(bf16[32,32,128]{2,1,0:T(8,128)(2,1)} %f_ref.1) | copy-start | bytes 786436
  2.7 0.8 %copy-start.2 = (s32[32,256]{1,0:T(8,128)S(1)}, s32[32,256]{1,0:T(8,128)}, u32[]{:S(2)}) copy-start(s32[32,256]{1,0:T(8,128)} %y_ref.1) | copy-start | bytes 98308

commit v3 on v2

--- a/solution.py
+++ b/solution.py
@@ -84,25 +84,40 @@
 
 def pair_up(h, d, segs):
     n, sub, lanes = h.shape
-    low = half_lanes((1, sub, lanes))
+    tile = 2 * sub
+    pack = lambda v: v.reshape(-1, tile, lanes).astype(jnp.bfloat16)
+    turn = lambda v: pltpu.roll(v, lanes // 2, 2)
+    shape = (1, tile, lanes)
+    low = half_lanes(shape)
+    row = lax.broadcasted_iota(jnp.int32, shape, 1)
     if d * segs < sub:
-        first = lax.broadcasted_iota(jnp.int32, (1, sub, lanes), 1) < sub // 2
-        other = pltpu.roll(pltpu.roll(h, sub // 2, 1), lanes // 2, 2)
-        return jnp.where(first == low, h, other)
-    g = d * segs // sub
-    turned = pltpu.roll(h, lanes // 2, 2)
-    groups = n // g
+        keep = (row % sub < sub // 2) == low
+        other = pltpu.roll(h, sub // 2, 1)
+        even = jnp.where(keep, pack(h), turn(pack(other)))
+        odd = jnp.where(keep, pack(h[1 : n - 1]), turn(pack(other[1 : n - 1])))
+        return odd, even
+    if d * segs < tile:
+        keep = (row < sub) == low
+        full = jnp.concatenate([h[:1], h, h[n - 1 :]], axis=0)
+        swapped = jnp.concatenate([full[i ^ 1 : (i ^ 1) + 1] for i in range(n + 2)], axis=0)
+        own = jnp.where(keep, pack(full), turn(pack(swapped)))
+        return own, own
+    v = pack(h)
+    turned = turn(v)
+    g = d * segs // tile
+    groups = v.shape[0] // g
     at = lambda x, m: x[m * g : (m + 1) * g]
     out = []
     for i in range((groups + 2) // 2):
-        u, v = 2 * i - 1, 2 * i
+        u, w = 2 * i - 1, 2 * i
         if i == 0:
-            out += [at(turned, v), at(h, v)]
-        elif v == groups:
-            out += [at(h, u), at(turned, u)]
+            out += [at(turned, w), at(v, w)]
+        elif w == groups:
+            out += [at(v, u), at(turned, u)]
         else:
-            out += [jnp.where(low, at(h, u), at(turned, v)), jnp.where(low, at(turned, u), at(h, v))]
-    return jnp.concatenate(out, axis=0)
+            out += [jnp.where(low, at(v, u), at(turned, w)), jnp.where(low, at(turned, u), at(v, w))]
+    own = jnp.concatenate(out, axis=0)
+    return own, own
 
 
 def shift_segment(h, segs, down):
@@ -127,8 +142,14 @@
 
 
 def pixel_kernel(
-    layers, n_src, f_ref, w_ref, h_ref, tr_ref, b_ref, y_ref, pw_ref, as_ref, o_ref, *scratch
+    layers, n_src, f_arg, w_arg, h_arg, tr_arg, b_arg, y_arg, pw_arg, as_arg, o_ref, *scratch
 ):
+    given = (f_arg, w_arg, h_arg, tr_arg, b_arg, y_arg, pw_arg, as_arg)
+    *scratch, f_ref, w_ref, h_ref, tr_ref, b_ref, y_ref, pw_ref, as_ref, ls = scratch
+    local = (f_ref, w_ref, h_ref, tr_ref, b_ref, y_ref, pw_ref, as_ref)
+    fetch = [pltpu.make_async_copy(a, b, ls.at[i]) for i, (a, b) in enumerate(zip(given, local))]
+    for copy in fetch:
+        copy.start()
     first, bufs = scratch[0], (scratch[1 : layers + 1], scratch[layers + 1 : 2 * layers + 1])
     got, wraw, pbuf, mbuf, wide, acc, sbuf, obuf, stage, rowbuf, t_ref, m_ref = scratch[2 * layers + 1 : 2 * layers + 13]
     fs, fr, es, er, ws, wr, ys, yr, vs, vr, ps, pr, ms, mr, os, orr = scratch[2 * layers + 13 :]
@@ -152,15 +173,7 @@
                     )
     pl.semaphore_signal(barrier, inc=1, device_id={"grp": 1 - gp}, device_id_type=MESH)
     ch = lanes // 2
-    planes2 = h_ref.shape[0]
-    ia = lax.broadcasted_iota(jnp.int32, (planes2, planes2), 0)
-    ib = lax.broadcasted_iota(jnp.int32, (planes2, planes2), 1)
-    column = jnp.sum(jnp.where(ia == ib, tr_ref[...], 0.0), axis=1, keepdims=True)
-    pbuf[0, :planes2, :] = jnp.concatenate(
-        [h_ref[...].astype(jnp.float32), jnp.broadcast_to(column, (planes2, ch))], axis=1)
-    bias_half = 0.5 * b_ref[...]
-    pbuf[0, planes2 : planes2 + layers, :] = jnp.concatenate([bias_half, bias_half], axis=1)
-
+    fetch[0].wait()
     part, strip, block = f_ref.shape
     for ci in range(part):
         rowbuf[ci * strip : (ci + 1) * strip, :] = f_ref[ci].astype(jnp.float32)
@@ -188,11 +201,23 @@
             base + 8 * x8 * half_rows : base + 8 * (x8 + 1) * half_rows, :
         ].reshape(8, half_rows, lanes).astype(t_ref.dtype)
 
+    fetch[1].wait()
     per = layers // 2
     for l in range(layers):
         for i, (one, two) in enumerate(((1, 0), (4, 3), (7, 6), (2, 5), (8, None))):
             other = jnp.zeros((ch, ch), w_ref.dtype) if two is None else w_ref[l, two]
             wraw[0, l // per, (l % per) * 5 + i] = jnp.concatenate([w_ref[l, one], other], axis=1)
+
+    for copy in fetch[2:]:
+        copy.wait()
+    planes2 = h_ref.shape[0]
+    ia = lax.broadcasted_iota(jnp.int32, (planes2, planes2), 0)
+    ib = lax.broadcasted_iota(jnp.int32, (planes2, planes2), 1)
+    column = jnp.sum(jnp.where(ia == ib, tr_ref[...], 0.0), axis=1, keepdims=True)
+    pbuf[0, :planes2, :] = jnp.concatenate(
+        [h_ref[...].astype(jnp.float32), jnp.broadcast_to(column, (planes2, ch))], axis=1)
+    bias_half = 0.5 * b_ref[...]
+    pbuf[0, planes2 : planes2 + layers, :] = jnp.concatenate([bias_half, bias_half], axis=1)
 
     pl.semaphore_wait(barrier, 4 * n_src)
 
@@ -404,6 +429,25 @@
 
     total = jnp.sum(pw_ref[...], axis=1, keepdims=True)
 
+    low_tile = half_lanes((1, 16, lanes))
+    outside_tiles = (slots // 2 - own_cols // 4) * segs // 16
+
+    def bordered(v):
+        n = v.shape[0]
+        missing = mrows // 16 - n
+        zero = jnp.zeros((), v.dtype)
+        if missing:
+            half = lax.broadcasted_iota(jnp.int32, (1, 16, lanes), 1) < 8
+            left = [jnp.where(at_left, zero, v[: outside_tiles - 1]),
+                    jnp.where(at_left & half, zero, v[outside_tiles - 1 : outside_tiles])]
+            right = [jnp.where(at_right & jnp.logical_not(half), zero, v[n - outside_tiles : n - outside_tiles + 1]),
+                     jnp.where(at_right, zero, v[n - outside_tiles + 1 :])]
+            middle = [v[outside_tiles : n - outside_tiles]]
+            return jnp.concatenate(left + middle + right, axis=0)
+        return jnp.concatenate(
+            [jnp.where(at_left, zero, v[:outside_tiles]), v[outside_tiles : n - outside_tiles],
+             jnp.where(at_right, zero, v[n - outside_tiles :])], axis=0)
+
     def store_next(dst, h, y, d):
         wider = 2 * d
         places = [(y, h)]
@@ -412,17 +456,17 @@
         if y < wider:
             places.append((y + span, shift_segment(h, segs, False)))
         for yy, v in places:
-            v = pair_up(v, d, segs)
-            n = v.shape[0]
-            out = (slots // 2 - own_cols // 4) * segs // 8
-            v = jnp.concatenate(
-                [jnp.where(at_left, 0.0, v[:out]), v[out : n - out], jnp.where(at_right, 0.0, v[n - out :])],
-                axis=0)
-            g = wider * segs // 8
-            near = jnp.where(low_lanes, v[2 * g :], v[: n - 2 * g])
-            own = v[g : n - g]
-            dst[yy + wider, :, :lanes] = own.reshape(-1, lanes).astype(dst.dtype)
-            dst[yy + wider, :, lanes:] = near.reshape(-1, lanes).astype(dst.dtype)
+            own, around = pair_up(v, d, segs)
+            around = bordered(around)
+            if own.shape[0] != around.shape[0]:
+                own = bordered(own)
+                near = jnp.where(low_tile, around[1:], around[:-1])
+            else:
+                g = wider * segs // 16
+                own = around[g : around.shape[0] - g]
+                near = jnp.where(low_tile, around[2 * g :], around[: around.shape[0] - 2 * g])
+            dst[yy + wider, :, :lanes] = own.reshape(-1, lanes)
+            dst[yy + wider, :, lanes:] = near.reshape(-1, lanes)
 
     def multiply(k, l, ys):
         d = 2**l
@@ -634,18 +678,20 @@
         spec((4, strip // 4, block), jnp.float32),
     ]
     dma = pltpu.SemaphoreType.DMA
+    given = (features, conv_weight[0], head_weight[0].T, transmission, conv_bias[0], layout, point_weight[None], assignment.reshape(1, -1))
     for count in (4, 4, 4, 4, n_src, n_src, n_src, n_src, n_src, n_src, n_src, n_src, 4, 2, 2 * n_src, 2 * n_src):
         scratch.append(dma((count,)))
+    scratch += [spec(a.shape, a.dtype) for a in given] + [dma((len(given),))]
     vmem = pl.BlockSpec(memory_space=pltpu.VMEM)
     out = pl.pallas_call(
         functools.partial(pixel_kernel, layers, n_src),
         out_shape=jax.ShapeDtypeStruct((planes2 // 2, 8, width // n_chan), jnp.float32),
-        in_specs=[vmem] * 8,
+        in_specs=[pl.BlockSpec(memory_space=pltpu.HBM)] * len(given),
         out_specs=vmem,
         scratch_shapes=scratch,
         compiler_params=pltpu.CompilerParams(
-            vmem_limit_bytes=26 * 2**20, collective_id=0, has_side_effects=True),
-    )(features, conv_weight[0], head_weight[0].T, transmission, conv_bias[0], layout, point_weight[None], assignment.reshape(1, -1))
+            vmem_limit_bytes=67043328 - 66 * 1024, collective_id=0, has_side_effects=True),
+    )(*given)
     return out[:, None]
 
 

time: 38.6 us -> 36.3 us (0.940)
  local copies, waits for them, and re-layouts: 4.11 us -> 1.47 us
  Pallas kernels: 34.2 us -> 34.6 us
    unnamed x17 -> x1, local copies, waits for them, and re-layouts: 4.11 us -> 1.47 us
    pallas_call x1, Pallas kernels: 34.2 us -> 34.6 us  [by_pixel(): pl.pallas_call(functools.partial(pixel_kernel, layers, n_src), out_shape=...]
where the time goes in v3:
time: 36.3 us; the launch traced here: 36.1 us
  Pallas kernels  34.6 us (95%)
  local copies, waits for them, and re-layouts  1.47 us (4%)
    pallas_call x1, Pallas kernels, by_pixel(): pl.pallas_call(functools.partial(pixel_kernel, layers, n_src), out_shape=...  34.6 us
    unnamed x1, local copies, waits for them, and re-layouts  1.47 us

profile of v3, /device:TPU:0, one launch (start us, length us, event | category | flops | bytes accessed | tf_op | source)
XLA Modules:
  0.0 36.1 jit_solution(17720564176025402571)
XLA Ops:
  0.0 34.6 %shard_map.82 = f32[8,8,256]{2,1,0:T(8,128)} custom-call(bf16[32,32,128]{2,1,0:T(8,128)(2,1)} %f_arg.1, bf16[4,9,64,64]{3,2,1,0:T(8,128)(2,1)} %bitcast.10, bf16[16,64]{1,0:T(8,128)(2,1)} %bitcast.12, f32[1,16]{1,0:T(1,128)} %tr_arg.1, f32[4,64]{1,0:T(4,128)} %bitcast.13, s32[32,256]{1,0:T(8,128)} %y_arg.1, f32[1,128]{1,0:T(1,128)} %bitcast.14, ...), custom_call_target="tpu_custom_call" | custom-call | tf_op jit(solution)/shard_map/pallas_call | solution.py:686
  34.6 1.5 %copy.11 = f32[8,1,8,256]{3,2,1,0:T(8,128)} copy(f32[8,1,8,256]{3,2,1,0:T(8,128)} %bitcast.11) | data formatting | bytes 131072
